TPU v7x, 256 devices: a whole 4x4x8 slice. The times are simulated.
256 devices in a mesh: shard: 64 (over x, y_hi, z), tensor: 4 (over y_lo, core).
Axes of the slice: x: 4, y: 4 (y_hi: 2, y_lo: 2; y = y_hi * 2 + y_lo), z: 8, core: 2. Of those that a mesh axis runs over, the one named last changes fastest.
Arguments:
- gradient: bfloat16 [768, 3072], P('shard', 'tensor'), may hold values from -0.47851562 to 0.47851562
- moment: float32 [768, 3072], P('shard', 'tensor'), may hold values from -0.48 to 0.48
- second_moment: float32 [768, 3072], P('shard', 'tensor'), may hold values from 0.0001 to 0.01
- stat_left: float32 [768, 768], P('shard', 'tensor'), as said below
- stat_right: float32 [3072, 3072], P('shard', 'tensor'), as said below
- basis_left: float32 [768, 768], P('shard', 'tensor'), as said below
- basis_right: float32 [3072, 3072], P('shard', 'tensor'), as said below
Outputs:
- update: float32 [768, 3072], P('shard', 'tensor')
- moment_new: float32 [768, 3072], P('shard', 'tensor')
- second_new: float32 [768, 3072], P('shard', 'tensor')
- stat_left_new: float32 [768, 768], P('shard', 'tensor')
- stat_right_new: float32 [3072, 3072], P('shard', 'tensor')
- basis_left_new: float32 [768, 768], P('shard', 'tensor')
- basis_right_new: float32 [3072, 3072], P('shard', 'tensor')
Inputs may be any that keep to these rules, and one draw needn't show every extreme that they name: `stat_left`: a symmetric matrix. `stat_right`: a symmetric matrix. `basis_left`: a square matrix of full rank. `basis_right`: a square matrix of full rank.
All inputs are finite; a program needn't handle non-finite values.
Results may differ from a plain program's by a relative error of at most 0.0018.
The roundings to bfloat16 on the way count: a program that leaves them out, or rounds other values in their place, can miss the bound.
Values may be sent and summed in bfloat16 or wider, within the bound.
No kernel may reach another device: no remote copies, remote signals or barrier semaphores. Data moves between devices by JAX's collectives and lax.ppermute only.
A program may use at most 64 MiB of HBM per device.

v0:
```python
import jax
import jax.numpy as jnp
from jax import lax
from jax.sharding import PartitionSpec as P

NS_ITERS = 2


def broadcast(array, axis, root):
    mine = lax.axis_index(axis) == root
    return lax.psum(jnp.where(mine, array, jnp.zeros_like(array)), axis)


def matmul(first_operand, second_operand):
    return jnp.dot(first_operand, second_operand, preferred_element_type=jnp.float32)


def contract_rows(first_operand, second_operand):
    return lax.dot_general(
        first_operand, second_operand, (((0,), (0,)), ((), ())), preferred_element_type=jnp.float32
    )


def contract_cols(first_operand, second_operand):
    return lax.dot_general(
        first_operand, second_operand, (((1,), (1,)), ((), ())), preferred_element_type=jnp.float32
    )


def owned_strip(column_panel, shard_index, tensor_index, strip_width):
    block_width = column_panel.shape[1]
    first_index = shard_index * strip_width
    owner_index = first_index // block_width
    offset = jnp.clip(first_index - tensor_index * block_width, 0, block_width - strip_width)
    return (owner_index, lax.dynamic_slice_in_dim(column_panel, offset, strip_width, 1))


def per_device(gradient, moment, second_moment, stat_left, stat_right, basis_left, basis_right):
    shard_index = lax.axis_index("shard")
    tensor_index = lax.axis_index("tensor")
    rows_left = gradient.shape[0]
    rows_right = stat_right.shape[0]
    block_left = stat_left.shape[1]
    block_hidden = gradient.shape[1]
    moment_new = 0.9 * moment + 0.1 * gradient.astype(jnp.float32)
    moment_half = moment_new.astype(jnp.bfloat16)
    basis_left_half = basis_left.astype(jnp.bfloat16)
    basis_right_half = basis_right.astype(jnp.bfloat16)
    grad_rows, moment_rows, basis_left_rows = (
        lax.all_gather(gradient, "tensor", axis=1, tiled=True),
        lax.all_gather(moment_half, "tensor", axis=1, tiled=True),
        lax.all_gather(basis_left_half, "tensor", axis=1, tiled=True),
    )
    left_columns, right_columns = (
        lax.all_gather(basis_left_half, "shard", axis=0, tiled=True),
        lax.all_gather(basis_right_half, "shard", axis=0, tiled=True),
    )
    full_gradient = lax.all_gather(grad_rows, "shard", axis=0, tiled=True)
    own_rows = lax.dynamic_slice_in_dim(full_gradient, tensor_index * block_left, block_left, 0)
    cross_left = contract_cols(grad_rows, own_rows)
    gradient_strip = lax.dynamic_slice_in_dim(
        full_gradient, shard_index * rows_right, rows_right, 1
    )
    own_columns = lax.dynamic_slice_in_dim(
        full_gradient, tensor_index * block_hidden, block_hidden, 1
    )
    cross_right = contract_rows(gradient_strip, own_columns)
    stat_left_new = 0.95 * stat_left + 0.05 * cross_left
    stat_right_new = 0.95 * stat_right + 0.05 * cross_right
    stat_left_rows, stat_right_rows = (
        lax.all_gather(stat_left_new.astype(jnp.bfloat16), "tensor", axis=1, tiled=True),
        lax.all_gather(stat_right_new.astype(jnp.bfloat16), "tensor", axis=1, tiled=True),
    )
    power_left = matmul(stat_left_rows, left_columns)
    power_right = matmul(stat_right_rows, right_columns)
    square_left, square_right = lax.psum(
        (jnp.sum(power_left * power_left), jnp.sum(power_right * power_right)), ("shard", "tensor")
    )
    iterate_left = power_left / jnp.sqrt(square_left + 1e-06)
    iterate_right = power_right / jnp.sqrt(square_right + 1e-06)
    for iteration in range(NS_ITERS):
        left_half = iterate_left.astype(jnp.bfloat16)
        right_half = iterate_right.astype(jnp.bfloat16)
        left_panel, right_panel = (
            lax.all_gather(left_half, "shard", axis=0, tiled=True),
            lax.all_gather(right_half, "shard", axis=0, tiled=True),
        )
        gram_left = contract_cols(left_half, left_panel)
        gram_right = contract_cols(right_half, right_panel)
        gram_left, gram_right = lax.psum((gram_left, gram_right), "tensor")
        gram_left_half = gram_left.astype(jnp.bfloat16)
        gram_right_half = gram_right.astype(jnp.bfloat16)
        iterate_left = 1.5 * iterate_left - 0.5 * matmul(gram_left_half, left_panel)
        iterate_right = 1.5 * iterate_right - 0.5 * matmul(gram_right_half, right_panel)
    rotated_grad = matmul(grad_rows, right_columns).astype(jnp.bfloat16)
    rotated_moment = matmul(moment_rows, right_columns).astype(jnp.bfloat16)
    grad_panel, moment_panel = (
        lax.all_gather(rotated_grad, "shard", axis=0, tiled=True),
        lax.all_gather(rotated_moment, "shard", axis=0, tiled=True),
    )
    owner_left, local_left = owned_strip(left_columns, shard_index, tensor_index, rows_left)
    basis_strip = broadcast(local_left, "tensor", owner_left)
    grad_turned = contract_rows(basis_strip, grad_panel)
    moment_turned = contract_rows(basis_strip, moment_panel)
    second_new = 0.95 * second_moment + 0.05 * grad_turned * grad_turned
    scaled = (moment_turned / (jnp.sqrt(second_new) + 1e-08)).astype(jnp.bfloat16)
    back_terms = contract_cols(scaled, right_columns)
    back_half = lax.psum_scatter(back_terms, "tensor", scatter_dimension=1, tiled=True).astype(
        jnp.bfloat16
    )
    back_panel = lax.all_gather(back_half, "shard", axis=0, tiled=True)
    update = matmul(basis_left_rows, back_panel)
    return (
        update,
        moment_new,
        second_new,
        stat_left_new,
        stat_right_new,
        iterate_left,
        iterate_right,
    )


def solution(mesh):
    return jax.shard_map(
        per_device,
        mesh=mesh,
        in_specs=(
            P("shard", "tensor"),
            P("shard", "tensor"),
            P("shard", "tensor"),
            P("shard", "tensor"),
            P("shard", "tensor"),
            P("shard", "tensor"),
            P("shard", "tensor"),
        ),
        out_specs=(
            P("shard", "tensor"),
            P("shard", "tensor"),
            P("shard", "tensor"),
            P("shard", "tensor"),
            P("shard", "tensor"),
            P("shard", "tensor"),
            P("shard", "tensor"),
        ),
        check_vma=False,
    )
```

profile of v0, /device:TPU:1, one launch (start us, length us, event | category | flops | bytes accessed | tf_op | source)
XLA Modules:
  0.0 1062.2 jit_solution(13101491253910753219)
XLA Ops:
  7.2 1.6 convert_element_type.57
  8.9 9.0 all_gather.49
  18.0 124.4 %all-gather.17.cloned.1.call-done = bf16[3072,768]{1,0:T(8,128)(2,1)} async-done(((bf16[48,768]{1,0:T(8,128)(2,1)}), bf16[3072,768]{1,0:T(8,128)(2,1)}) %all-gather.17.cloned.1.call-update) | async-done | bytes 4718608 | tf_op jit(solution)/shard_map/all_gather | solution.py:56
  142.4 3.7 fusion.14
  146.8 9.3 all_gather.46
  156.1 3.7 fusion.13
  159.9 154.4 %all-gather = bf16[64,12,192]{2,1,0:T(8,128)(2,1)S(1)} all-gather(bf16[1,12,192]{2,1,0:T(8,128)(2,1)S(1)} %get-tuple-element.16), channel_id=1, replica_groups=mesh['shard'=64,'tensor'=4] {'shard'}, dimensions={0}, use_global_device_ids=true | all-gather | bytes 299520 | tf_op jit(solution)/shard_map/all_gather | solution.py:55
  314.6 40.0 %psum.49 = bf16[768,12]{1,0:T(8,128)(2,1)S(1)} all-reduce(bf16[768,12]{1,0:T(8,128)(2,1)S(1)} %dynamic-slice_select_fusion), channel_id=1, replica_groups=mesh['shard'=64,'tensor'=4] {'tensor'}, use_global_device_ids=true, to_apply=%region_0.0 | all-reduce | flops 9216 | bytes 36864 | tf_op jit(solution)/shard_map/psum | solution.py:11
  354.6 7.6 reshape.25
  362.3 1.7 fusion.22
  364.0 5.3 all-gather.6
  369.4 2.6 fusion.47
  372.0 8.4 all_gather.57
  380.4 3.8 multiply_reduce_fusion
  384.2 12.6 %all-gather.25.cloned.1.call-done = bf16[64,12,768]{2,1,0:T(8,128)(2,1)} async-done(((bf16[1,12,768]{2,1,0:T(8,128)(2,1)}), bf16[64,12,768]{2,1,0:T(8,128)(2,1)}) %all-gather.25.cloned.1.call-update) | async-done | bytes 1179664 | tf_op jit(solution)/shard_map/all_gather | solution.py:98
  396.8 2.2 reshape.19
  399.4 114.2 %all-gather.23.cloned.1.call-done = bf16[64,12,768]{2,1,0:T(8,128)(2,1)} async-done(((bf16[1,12,768]{2,1,0:T(8,128)(2,1)}), bf16[64,12,768]{2,1,0:T(8,128)(2,1)}) %all-gather.23.cloned.1.call-update) | async-done | bytes 1179664 | tf_op jit(solution)/shard_map/all_gather | solution.py:99
  513.6 2.2 reshape.17
  515.9 4.6 fusion.15
  521.3 78.2 %all-reduce = (f32[]{:T(128)}, f32[]{:T(128)}) all-reduce(f32[]{:T(128)} %get-tuple-element.17, f32[]{:T(128)} %get-tuple-element.21), channel_id=1, replica_groups=mesh['shard'=64,'tensor'=4] {'shard','tensor'}, use_global_device_ids=true, to_apply=%region_3.0 | all-reduce | flops 2 | bytes 16 | tf_op jit(solution)/shard_map/psum | solution.py:76
  601.0 1.4 convert_bitcast_fusion
  603.2 151.2 %all-gather.7 = bf16[64,12,192]{2,1,0:T(8,128)(2,1)S(1)} all-gather(bf16[1,12,192]{2,1,0:T(8,128)(2,1)S(1)} %fusion.45), channel_id=1, replica_groups=mesh['shard'=64,'tensor'=4] {'shard'}, dimensions={0}, use_global_device_ids=true | all-gather | bytes 299520 | tf_op jit(solution)/shard_map/all_gather | solution.py:85
  754.9 3.9 fusion.49
  758.7 44.7 %all-reduce.5 = (bf16[12,768]{1,0:T(8,128)(2,1)S(1)}, bf16[48,3072]{1,0:T(8,128)(2,1)S(1)}) all-reduce(f32[12,768]{1,0:T(8,128)S(1)} %fusion.43, f32[48,3072]{1,0:T(8,128)S(1)} %fusion.49), channel_id=1, replica_groups=mesh['shard'=64,'tensor'=4] {'tensor'}, use_global_device_ids=true, to_apply=%region_4.0 | all-reduce | flops 156672 | bytes 940032 | tf_op jit(solution)/shard_map/psum | solution.py:90
  803.5 3.9 fusion.48
  807.4 6.0 all-gather.4
  813.5 26.7 %all-gather.27.cloned.1.call-done = bf16[64,12,768]{2,1,0:T(8,128)(2,1)} async-done(((bf16[1,12,768]{2,1,0:T(8,128)(2,1)}), bf16[64,12,768]{2,1,0:T(8,128)(2,1)}) %all-gather.27.cloned.1.call-update) | async-done | bytes 1179664 | tf_op jit(solution)/shard_map/all_gather | solution.py:111
  840.3 2.2 reshape.21
  843.6 152.9 %all-gather.8 = bf16[64,12,192]{2,1,0:T(8,128)(2,1)S(1)} all-gather(bf16[1,12,192]{2,1,0:T(8,128)(2,1)S(1)} %convert_bitcast_fusion.2), channel_id=1, replica_groups=mesh['shard'=64,'tensor'=4] {'shard'}, dimensions={0}, use_global_device_ids=true | all-gather | bytes 299520 | tf_op jit(solution)/shard_map/all_gather | solution.py:85
  996.9 3.8 fusion.50
  1000.8 49.9 %all-reduce.6 = (bf16[12,768]{1,0:T(8,128)(2,1)S(1)}, bf16[48,3072]{1,0:T(8,128)(2,1)S(1)}) all-reduce(f32[12,768]{1,0:T(8,128)S(1)} %fusion.38, f32[48,3072]{1,0:T(8,128)S(1)} %fusion.50), channel_id=1, replica_groups=mesh['shard'=64,'tensor'=4] {'tensor'}, use_global_device_ids=true, to_apply=%region_5.0 | all-reduce | flops 156672 | bytes 940032 | tf_op jit(solution)/shard_map/psum | solution.py:90
  1051.5 3.9 fusion.4
  (61 shorter events, 6.2 us)
Async XLA Ops:
  7.2 139.0 %copy-start.4 = (bf16[12,768]{1,0:T(8,128)(2,1)S(1)}, bf16[12,768]{1,0:T(8,128)(2,1)}, u32[]{:S(2)}) copy-start(bf16[12,768]{1,0:T(8,128)(2,1)} %param.7) | copy-start | bytes 55300
  7.2 139.0 %copy-start.7 = (f32[12,768]{1,0:T(8,128)S(1)}, f32[12,768]{1,0:T(8,128)}, u32[]{:S(2)}) copy-start(f32[12,768]{1,0:T(8,128)} %param.8) | copy-start | bytes 110596
  7.2 135.2 %all-gather.17.cloned.1.call-start = ((), (), s32[]{:S(2)}) async-start(), calls=%async_computation.1 | async-start | bytes 4792320 | tf_op jit(solution)/shard_map/all_gather | solution.py:56
  8.8 345.8 %all-gather.29.cloned.1.call-start = ((), (), s32[]{:S(2)}) async-start(), calls=%async_computation.8 | async-start | bytes 6389760 | tf_op jit(solution)/shard_map/all_gather | solution.py:58
  17.9 141.9 %copy-start.9 = (f32[12,192]{1,0:T(8,128)S(1)}, f32[12,192]{1,0:T(8,128)}, u32[]{:S(2)}) copy-start(f32[12,192]{1,0:T(8,128)} %param.12) | copy-start | bytes 27652
  17.9 378.9 %all-gather.25.cloned.1.call-start = ((), (), s32[]{:S(2)}) async-start(), calls=%async_computation.6 | async-start | bytes 1597440 | tf_op jit(solution)/shard_map/all_gather | solution.py:98
  146.1 367.5 %all-gather.23.cloned.1.call-start = ((), (), s32[]{:S(2)}) async-start(), calls=%async_computation.5 | async-start | bytes 1597440 | tf_op jit(solution)/shard_map/all_gather | solution.py:99
  159.8 441.2 %reduce-scatter.2.cloned.1.call-start = ((), (), s32[]{:S(2)}) async-start(), calls=%async_computation.2 | async-start | bytes 245760 | tf_op jit(solution)/shard_map/reduce_scatter | solution.py:108
  354.6 7.7 copy-start
  354.6 7.7 copy-start.8
  354.6 14.8 %copy-start.3 = (f32[48,768]{1,0:T(8,128)S(1)}, f32[48,768]{1,0:T(8,128)}, u32[]{:S(2)}) copy-start(f32[48,768]{1,0:T(8,128)} %param.11) | copy-start | bytes 442372
  364.0 35.1 %copy-start.5 = (f32[12,192]{1,0:T(8,128)}, f32[12,192]{1,0:T(8,128)S(1)}, u32[]{:S(2)}) copy-start(f32[12,192]{1,0:T(8,128)S(1)} %fusion.22) | copy-start | bytes 27652
  369.4 29.7 %copy-start.6 = (f32[12,768]{1,0:T(8,128)S(1)}, f32[12,768]{1,0:T(8,128)}, u32[]{:S(2)}) copy-start(f32[12,768]{1,0:T(8,128)} %param.9) | copy-start | bytes 110596
  399.4 121.9 %copy-start.2 = (f32[12,768]{1,0:T(8,128)}, f32[12,768]{1,0:T(8,128)S(1)}, u32[]{:S(2)}) copy-start(f32[12,768]{1,0:T(8,128)S(1)} %fusion.31) | copy-start | bytes 110596
  520.5 234.4 %all-gather.19.cloned.1.call-start = ((), (), s32[]{:S(2)}) async-start(), calls=%async_computation.3 | async-start | bytes 4792320 | tf_op jit(solution)/shard_map/all_gather | solution.py:86
  600.9 239.4 %all-gather.27.cloned.1.call-start = ((), (), s32[]{:S(2)}) async-start(), calls=%async_computation.7 | async-start | bytes 1597440 | tf_op jit(solution)/shard_map/all_gather | solution.py:111
  602.4 394.5 %all-gather.21.cloned.1.call-start = ((), (), s32[]{:S(2)}) async-start(), calls=%async_computation.4 | async-start | bytes 4792320 | tf_op jit(solution)/shard_map/all_gather | solution.py:86
  807.4 189.5 %copy-start.1 = (bf16[48,768]{1,0:T(8,128)(2,1)S(1)}, bf16[48,768]{1,0:T(8,128)(2,1)}, u32[]{:S(2)}) copy-start(bf16[48,768]{1,0:T(8,128)(2,1)} %get-tuple-element.23) | copy-start | bytes 221188
Sparse Core Ops, SparseCore 0:
  12.2 130.0 all-gather.16
  146.0 134.3 all-gather.28
  284.7 112.0 all-gather.24
  400.9 112.6 all-gather.22
  520.6 20.4 reduce-scatter.1
  601.0 122.2 all-gather.18
  727.6 112.6 all-gather.26
  844.5 126.5 all-gather.20
where the time goes:
time: 1060 us
  blocking collectives  709 us (67%)
  waiting for transfers between devices  278 us (26%)
  matrix products  38.9 us (4%)
  between operations  15.9 us (2%)
  local copies, waits for them, and re-layouts  15.2 us (1%)
    all_gather x2, blocking collectives, per_device(): lax.all_gather(left_half, 'shard', axis=0, tiled=True)  304 us
    all_gather x1, blocking collectives, per_device(): lax.all_gather(basis_left_half, 'shard', axis=0, tiled=True)  154 us
    all_gather x1, waiting for transfers between devices, per_device(): lax.all_gather(basis_right_half, 'shard', axis=0, tiled=True)  124 us
    all_gather x1, waiting for transfers between devices, per_device(): lax.all_gather(rotated_moment, 'shard', axis=0, tiled=True)  114 us
    psum x2, blocking collectives, per_device(): gram_left, gram_right = lax.psum((gram_left, gram_right), 'tensor')  94.7 us
    psum x1, blocking collectives, per_device(): lax.psum((jnp.sum(power_left * power_left), jnp.sum(power_right * power_r...  78.2 us
    psum x1, blocking collectives, broadcast(): return lax.psum(jnp.where(mine, array, jnp.zeros_like(array)), axis)  40 us
    all_gather x1, waiting for transfers between devices, per_device(): back_panel = lax.all_gather(back_half, 'shard', axis=0, tiled=True)  26.7 us
  transfers between devices with their start and end apart: 8, of which 4 were waited for; matrix products, arithmetic and copies ran while one was open for 4% of the time, Pallas kernels for 0%

commit v1 on v0

v1 whole, which is shorter than its diff:
```python
import jax
import jax.numpy as jnp
from jax import lax
from jax.sharding import Mesh, PartitionSpec as P

BF = jnp.bfloat16
F32 = jnp.float32

AXES = ("x", "yh", "zq", "zp", "yl", "c")
SIZES = (4, 2, 4, 2, 2, 2)
SIZE = dict(zip(AXES, SIZES))
DEPTH = ("zq", "zp")
PLANE = ("x", "yh")
TENSOR = ("yl", "c")
ROWS = ("x", "yh", "zp")
COLS = ("yl", "zq")


def group(axes):
    total = 1
    for axis in axes:
        total *= SIZE[axis]
    return total


def exchange(pieces, axes):
    return lax.all_to_all(pieces, axes, 0, 0, tiled=True)


def gather(array, axes):
    return exchange(jnp.broadcast_to(array[None], (group(axes),) + array.shape), axes)


def swap_core(array):
    return lax.ppermute(array, "c", ((0, 1), (1, 0)))


def in_order(core, own, other):
    return jnp.stack([jnp.where(core == 0, own, other), jnp.where(core == 0, other, own)])


def grid_permute(array, flip):
    pairs = []
    for high in range(2):
        for low in range(2):
            for core in range(2):
                pairs.append(((high * 2 + low) * 2 + core, (core * 2 + (low ^ flip)) * 2 + high))
    return lax.ppermute(array, ("zq", "c"), pairs)


def to_grid(array, low):
    width = array.shape[1] // 2
    left, right = array[:, :width], array[:, width:]
    same = grid_permute(jnp.where(low == 0, left, right), 0)
    other = grid_permute(jnp.where(low == 0, right, left), 1)
    return in_order(low, same, other)


def to_natural(array, low):
    same = grid_permute(jnp.where(low == 0, array[0], array[1]), 0)
    other = grid_permute(jnp.where(low == 0, array[1], array[0]), 1)
    return jnp.concatenate(
        [jnp.where(low == 0, same, other), jnp.where(low == 0, other, same)], axis=1
    )


def dot(first, second, dims):
    return lax.dot_general(first, second, (dims, ((), ())), preferred_element_type=F32)


def contract_blocks(blocks, panel):
    return dot(blocks, panel, ((0, 2), (0, 1)))


def natural_rows(gathered):
    _, _, _, rows, width = gathered.shape
    parts = gathered.reshape(2, 4, 2, 2, 2, rows, width)
    return parts.transpose(1, 2, 0, 4, 3, 5, 6).reshape(8, 8 * rows, width)


def per_device(gradient, moment, second_moment, stat_left, stat_right, basis_left, basis_right):
    place = {axis: lax.axis_index(axis) for axis in AXES}
    core = place["c"]
    low = place["zq"] % 2
    depth = place["zq"] * 2 + place["zp"]
    shard = place["x"] * 16 + place["yh"] * 8 + depth
    tensor = place["yl"] * 2 + core
    rows, width = gradient.shape
    rows_right = stat_right.shape[0]
    width_left = stat_left.shape[1]
    order = 64 * rows
    half = width // 2

    moment_new = 0.9 * moment + 0.1 * gradient.astype(F32)
    moment_half = moment_new.astype(BF)
    left_half = basis_left.astype(BF)
    right_half = basis_right.astype(BF)

    grad_deep = gather(gradient, DEPTH).reshape(8 * rows, width)
    strips = jnp.stack(
        [
            lax.dynamic_slice_in_dim(grad_deep, half * side + rows_right * depth, rows_right, 1)
            for side in range(2)
        ]
    )
    strips = lax.ppermute(
        strips,
        ("x", "yl", "c"),
        [(first * 4 + second, second * 4 + first) for first in range(4) for second in range(4)],
    )
    strips = exchange(
        jnp.broadcast_to(strips[:, None], (2, 4) + strips.shape[1:]).reshape(
            8, 8 * rows, rows_right
        ),
        ("yh",) + TENSOR,
    )
    strip = (
        strips.reshape(2, 4, 8 * rows, rows_right).transpose(1, 0, 2, 3).reshape(order, rows_right)
    )
    grad_panel = gather(grad_deep, PLANE).reshape(order, width)

    basis_grid = to_grid(right_half, low).reshape(2 * rows_right, half)
    basis_own = gather(basis_grid, ROWS)
    basis_other = swap_core(basis_own)
    basis_panel = natural_rows(
        in_order(core, basis_own, basis_other).reshape(2, 16, 2, rows_right, half)
    )

    cross_right = dot(strip, grad_panel, ((0,), (0,)))
    stat_right_new = 0.95 * stat_right + 0.05 * cross_right
    stat_grid = to_grid(stat_right_new.astype(BF), low).reshape(2 * rows_right, half)
    stat_rows = gather(stat_grid, COLS)
    power = contract_blocks(stat_rows, basis_panel)

    def gather_sum(value, axes):
        return jnp.sum(gather(jnp.full((8, 128), value, F32), axes)[:, 0, 0])

    square = gather_sum(gather_sum(jnp.sum(power * power), ROWS + ("c",)), COLS) + 1e-06
    iterate = power
    for iteration in range(2):
        block = iterate.astype(BF)
        own = gather(block, ROWS).reshape(16 * block.shape[0], half)
        other = swap_core(own)
        panel = jnp.concatenate([own, other]).reshape(8, half, half)
        parts = jnp.stack(
            [dot(block, panel[piece], ((1,), (1,))).astype(BF) for piece in range(8)]
        )
        gram = jnp.sum(exchange(parts, COLS).astype(F32), axis=0)
        if iteration == 0:
            gram = gram / square
        gram_rows = gather(gram.astype(BF), COLS)
        iterate = 1.5 * iterate - 0.5 * contract_blocks(gram_rows, panel)
        if iteration == 0:
            iterate = iterate / jnp.sqrt(square)
    basis_right_new = to_natural(iterate.reshape(2, rows_right, half), low)

    left_rows = gather(left_half, TENSOR).transpose(1, 0, 2).reshape(rows, order)
    left_deep = gather(left_rows, DEPTH).reshape(8 * rows, order)
    left = gather(left_deep, PLANE).reshape(order, order)
    cross_parts = dot(gradient, grad_panel, ((1,), (1,)))
    cross_parts = cross_parts.reshape(rows, 4, width_left).transpose(1, 0, 2)
    cross_left = jnp.sum(exchange(cross_parts, TENSOR), axis=0)
    stat_left_new = 0.95 * stat_left + 0.05 * cross_left
    stat_full = gather(stat_left_new.astype(BF), TENSOR).transpose(1, 0, 2).reshape(rows, order)
    stat_full = gather(stat_full, DEPTH).reshape(8 * rows, order)
    stat_full = gather(stat_full, PLANE).reshape(order, order)
    power_left = dot(stat_full, left, ((1,), (0,)))
    iterate_left = power_left / jnp.sqrt(jnp.sum(power_left * power_left) + 1e-06)
    half_left = iterate_left.astype(BF)
    gram_left = dot(half_left, half_left, ((1,), (1,))).astype(BF)
    iterate_left = 1.5 * iterate_left - 0.5 * dot(gram_left, half_left, ((1,), (0,)))
    half_left = iterate_left.astype(BF)
    own_left = lax.dynamic_slice_in_dim(half_left, shard * rows, rows, 0)
    gram_own = dot(own_left, half_left, ((1,), (1,))).astype(BF)
    columns_left = lax.dynamic_slice_in_dim(half_left, tensor * width_left, width_left, 1)
    block_left = lax.dynamic_slice(
        iterate_left, (shard * rows, tensor * width_left), (rows, width_left)
    )
    basis_left_new = 1.5 * block_left - 0.5 * dot(gram_own, columns_left, ((1,), (0,)))

    both = to_grid(jnp.concatenate([gradient, moment_half]), low)
    both_rows = gather(both.reshape(4 * rows, half), COLS)
    rotated = contract_blocks(both_rows, basis_panel).astype(BF)

    def gather_rows(array):
        own = gather(array, ROWS)
        both = in_order(core, own, swap_core(own))
        return natural_rows(both).reshape(order, array.shape[2])

    rotated = rotated.reshape(2, 2, rows, half).transpose(0, 2, 1, 3).reshape(2, rows, 2 * half)
    rotated = gather_rows(rotated)
    starts = [
        rows * (16 * place["x"] + 8 * place["yh"] + 2 * (2 * core + side) + place["zp"])
        for side in range(2)
    ]
    left_columns = jnp.concatenate(
        [lax.dynamic_slice_in_dim(left, start, rows, 1) for start in starts], axis=1
    )
    left_own = jnp.concatenate([lax.dynamic_slice_in_dim(left, start, rows, 0) for start in starts])
    turned = dot(left_columns, rotated, ((0,), (0,)))
    grad_turned, moment_turned = turned[:, :half], turned[:, half:]
    second_grid = to_grid(second_moment, low).reshape(2 * rows, half)
    second_new = 0.95 * second_grid + 0.05 * grad_turned * grad_turned
    scaled = (moment_turned / (jnp.sqrt(second_new) + 1e-08)).astype(BF)
    back = jnp.stack([dot(scaled, basis_panel[piece], ((1,), (1,))) for piece in range(8)])
    back = jnp.sum(exchange(back, COLS), axis=0).astype(BF)
    back = gather_rows(back.reshape(2, rows, half))
    update = dot(left_own, back, ((1,), (0,)))
    result = jnp.concatenate(
        [update.reshape(2, rows, half), second_new.reshape(2, rows, half)], axis=1
    )
    result = to_natural(result, low)
    return (
        result[:rows],
        moment_new,
        result[rows:],
        stat_left_new,
        stat_right_new,
        basis_left_new,
        basis_right_new,
    )


def solution(mesh):
    parts = Mesh(mesh.devices.reshape(SIZES), AXES)
    spec = P(("x", "yh", "zq", "zp"), TENSOR)
    return jax.shard_map(
        per_device,
        mesh=parts,
        in_specs=(spec,) * 7,
        out_specs=(spec,) * 7,
        check_vma=False,
    )
```

time: 1060 us -> 459 us (0.43)
  blocking collectives: 709 us -> 8.71 us
  starting transfers between devices: 0.33 us -> 180 us
  waiting for transfers between devices: 278 us -> 157 us
  local copies, waits for them, and re-layouts: 15.2 us -> 39.8 us
  other arithmetic: 4.42 us -> 18.4 us
  between operations: 15.9 us -> 2.86 us
    all_gather x8 -> x0, blocking collectives: 496 us -> none  [the longest x2 304 us: per_device(): lax.all_gather(left_half, 'shard', axis=0, tiled=True)]
    all_gather x7 -> x0, waiting for transfers between devices: 278 us -> none  [the longest x1 124 us: per_device(): lax.all_gather(basis_right_half, 'shard', axis=0, tiled=True)]
    psum x4 -> x0, blocking collectives: 213 us -> none  [the longest x2 94.7 us: per_device(): gram_left, gram_right = lax.psum((gram_left, gram_right), 'tensor')]
    all_to_all x0 -> x23, waiting for transfers between devices: none -> 127 us  [exchange(): return lax.all_to_all(pieces, axes, 0, 0, tiled=True)]
    all_to_all x0 -> x23, starting transfers between devices: none -> 121 us  [exchange(): return lax.all_to_all(pieces, axes, 0, 0, tiled=True)]
    ppermute x0 -> x18, starting transfers between devices: none -> 58.7 us  [the longest x12 36.8 us: grid_permute(): return lax.ppermute(array, ('zq', 'c'), pairs)]
    ppermute x0 -> x18, waiting for transfers between devices: none -> 29.6 us  [the longest x12 26 us: grid_permute(): return lax.ppermute(array, ('zq', 'c'), pairs)]
    broadcast_in_dim x0 -> x24, local copies, waits for them, and re-layouts: none -> 19.2 us  [the longest x23 18.5 us: gather(): jnp.broadcast_to(array[None], (group(axes),) + array.shape)]
  transfers between devices with their start and end apart: 8 -> 41, of which waited for: 4 -> 26; matrix products, arithmetic and copies ran while one was open for 4% -> 19% of each run, Pallas kernels for 0% -> 0%
where the time goes in v1:
time: 459 us; the launch traced here: 456 us
  starting transfers between devices  180 us (39%)
  waiting for transfers between devices  157 us (34%)
  matrix products  49.2 us (11%)
  local copies, waits for them, and re-layouts  39.8 us (9%)
  other arithmetic  18.4 us (4%)
  blocking collectives  8.71 us (2%)
    all_to_all x23, waiting for transfers between devices, exchange(): return lax.all_to_all(pieces, axes, 0, 0, tiled=True)  127 us
    all_to_all x23, starting transfers between devices, exchange(): return lax.all_to_all(pieces, axes, 0, 0, tiled=True)  121 us
    dot_general x35, matrix products, dot(): lax.dot_general(first, second, (dims, ((), ())), preferred_element_type=F32)  49.2 us
    ppermute x12, starting transfers between devices, grid_permute(): return lax.ppermute(array, ('zq', 'c'), pairs)  36.8 us
    ppermute x12, waiting for transfers between devices, grid_permute(): return lax.ppermute(array, ('zq', 'c'), pairs)  26 us
    ppermute x5, starting transfers between devices, swap_core(): return lax.ppermute(array, 'c', ((0, 1), (1, 0)))  19.5 us
    broadcast_in_dim x23, local copies, waits for them, and re-layouts, gather(): jnp.broadcast_to(array[None], (group(axes),) + array.shape)  18.5 us
  transfers between devices with their start and end apart: 41, of which 26 were waited for; matrix products, arithmetic and copies ran while one was open for 19% of the time, Pallas kernels for 0%

profile of v1, /device:TPU:1, one launch (start us, length us, event | category | flops | bytes accessed | tf_op | source)
XLA Modules:
  0.0 455.8 jit_solution(12497848744793844667)
XLA Ops:
  1.4 8.7 %all_to_all.120 = bf16[4,12,192]{2,1,0:T(8,128)(2,1)S(1)} all-to-all(bf16[4,12,192]{2,1,0:T(8,128)(2,1)S(1)} %broadcast_in_dim.54), channel_id=1, replica_groups=mesh['x'=4,'yh'=2,'zq'=4,'zp'=2,'yl'=2,'c'=2] {'yl','c'}, dimensions={0} | all-to-all | bytes 36864 | tf_op jit(solution)/shard_map/all_to_all | solution.py:27
  11.5 6.8 %all-to-all-start.8 = ((bf16[8,12,768]{2,1,0:T(8,128)(2,1)}), bf16[8,12,768]{2,1,0:T(8,128)(2,1)S(1)}, u32[]{:S(2)}, u32[]{:S(2)}) async-start(bf16[8,12,768]{2,1,0:T(8,128)(2,1)} %broadcast_in_dim.128), calls=%async_computation.8 | async-start | bytes 393216 | tf_op jit(solution)/shard_map/all_to_all | solution.py:27
  18.4 8.9 %all-to-all-done.8 = bf16[8,12,768]{2,1,0:T(8,128)(2,1)S(1)} async-done(((bf16[8,12,768]{2,1,0:T(8,128)(2,1)}), bf16[8,12,768]{2,1,0:T(8,128)(2,1)S(1)}, u32[]{:S(2)}, u32[]{:S(2)}) %all-to-all-start.8) | async-done | bytes 147488 | tf_op jit(solution)/shard_map/all_to_all | solution.py:27
  31.4 8.5 %all-to-all-done.1 = bf16[8,12,768]{2,1,0:T(8,128)(2,1)S(1)} async-done(((bf16[8,12,768]{2,1,0:T(8,128)(2,1)}), bf16[8,12,768]{2,1,0:T(8,128)(2,1)S(1)}, u32[]{:S(2)}, u32[]{:S(2)}) %all-to-all-start.1) | async-done | bytes 147488 | tf_op jit(solution)/shard_map/all_to_all | solution.py:27
  41.0 6.5 %all-to-all-start.9 = ((bf16[8,96,768]{2,1,0:T(8,128)(2,1)}), bf16[8,96,768]{2,1,0:T(8,128)(2,1)S(1)}, u32[]{:S(2)}, u32[]{:S(2)}) async-start(bf16[8,96,768]{2,1,0:T(8,128)(2,1)} %broadcast_in_dim.130), calls=%async_computation.9 | async-start | bytes 2359296 | tf_op jit(solution)/shard_map/all_to_all | solution.py:27
  48.2 5.9 %collective-permute-start = (bf16[24,384]{1,0:T(8,128)(2,1)S(1)}, bf16[24,384]{1,0:T(8,128)(2,1)S(1)}, u32[]{:S(2)}, u32[]{:S(2)}) collective-permute-start(bf16[24,384]{1,0:T(8,128)(2,1)S(1)} %get-tuple-element.57), channel_id=1, source_target_pairs={{0,0},{1,16},{8,8},{9,24},{16,1},{17,17},{24,9},{25,25},{2,2},{3,1... | collective-permute-start | bytes 55304 | tf_op jit(solution)/shard_map/ppermute | solution.py:48
  64.1 6.8 %all-to-all-start.11 = ((bf16[8,96,48]{1,2,0:T(8,128)(2,1)}), bf16[8,96,48]{1,2,0:T(8,128)(2,1)S(1)}, u32[]{:S(2)}, u32[]{:S(2)}) async-start(bf16[8,96,48]{1,2,0:T(8,128)(2,1)} %bitcast.45), calls=%async_computation.11 | async-start | bytes 196608 | tf_op jit(solution)/shard_map/all_to_all | solution.py:27
  87.4 8.2 %collective-permute-start.2 = (bf16[48,384]{1,0:T(8,128)(2,1)S(1)}, bf16[48,384]{1,0:T(8,128)(2,1)S(1)}, u32[]{:S(2)}, u32[]{:S(2)}) collective-permute-start(bf16[48,384]{1,0:T(8,128)(2,1)S(1)} %get-tuple-element.51), channel_id=1, source_target_pairs={{0,0},{1,16},{8,8},{9,24},{16,1},{17,17},{24,9},{25,25},{2,2},{3,1... | collective-permute-start | bytes 110600 | tf_op jit(solution)/shard_map/ppermute | solution.py:48
  95.7 5.5 %collective-permute-done.2 = bf16[48,384]{1,0:T(8,128)(2,1)S(1)} collective-permute-done((bf16[48,384]{1,0:T(8,128)(2,1)S(1)}, bf16[48,384]{1,0:T(8,128)(2,1)S(1)}, u32[]{:S(2)}, u32[]{:S(2)}) %collective-permute-start.2) | collective-permute-done | bytes 36896 | tf_op jit(solution)/shard_map/ppermute | solution.py:48
  109.9 6.8 %all-to-all-start.4 = ((bf16[16,96,384]{2,1,0:T(8,128)(2,1)}), bf16[16,96,384]{2,1,0:T(8,128)(2,1)S(1)}, u32[]{:S(2)}, u32[]{:S(2)}) async-start(bf16[16,96,384]{2,1,0:T(8,128)(2,1)} %broadcast_in_dim.124), calls=%async_computation.4 | async-start | bytes 2359296 | tf_op jit(solution)/shard_map/all_to_all | solution.py:27
  116.8 18.1 %all-to-all-done.4 = bf16[16,96,384]{2,1,0:T(8,128)(2,1)S(1)} async-done(((bf16[16,96,384]{2,1,0:T(8,128)(2,1)}), bf16[16,96,384]{2,1,0:T(8,128)(2,1)S(1)}, u32[]{:S(2)}, u32[]{:S(2)}) %all-to-all-start.4) | async-done | bytes 1179680 | tf_op jit(solution)/shard_map/all_to_all | solution.py:27
  160.7 8.3 %all-to-all-done.13 = bf16[8,12,768]{2,1,0:T(8,128)(2,1)S(1)} async-done(((bf16[8,12,768]{2,1,0:T(8,128)(2,1)}), bf16[8,12,768]{2,1,0:T(8,128)(2,1)S(1)}, u32[]{:S(2)}, u32[]{:S(2)}) %all-to-all-start.13) | async-done | bytes 147488 | tf_op jit(solution)/shard_map/all_to_all | solution.py:27
  176.8 13.6 %all-to-all-done.15 = bf16[8,96,384]{2,1,0:T(8,128)(2,1)S(1)} async-done(((bf16[8,96,384]{2,1,0:T(8,128)(2,1)}), bf16[8,96,384]{2,1,0:T(8,128)(2,1)S(1)}, u32[]{:S(2)}, u32[]{:S(2)}) %all-to-all-start.15) | async-done | bytes 589856 | tf_op jit(solution)/shard_map/all_to_all | solution.py:27
  191.5 6.6 %all-to-all-start.5 = ((bf16[16,2,12,768]{3,1,2,0:T(2,128)(2,1)}), bf16[16,2,12,768]{3,1,2,0:T(2,128)(2,1)}, u32[]{:S(2)}, u32[]{:S(2)}) async-start(bf16[16,2,12,768]{3,1,2,0:T(2,128)(2,1)} %broadcast_in_dim.126), calls=%async_computation.5 | async-start | bytes 1179648 | tf_op jit(solution)/shard_map/all_to_all | solution.py:27
  199.9 7.2 %all-to-all-done.5 = bf16[16,2,12,768]{3,1,2,0:T(2,128)(2,1)} async-done(((bf16[16,2,12,768]{3,1,2,0:T(2,128)(2,1)}), bf16[16,2,12,768]{3,1,2,0:T(2,128)(2,1)}, u32[]{:S(2)}, u32[]{:S(2)}) %all-to-all-start.5) | async-done | bytes 589856 | tf_op jit(solution)/shard_map/all_to_all | solution.py:27
  208.4 8.1 %all-to-all-start.18 = ((f32[32,8,128]{2,1,0:T(8,128)}), f32[32,8,128]{2,1,0:T(8,128)S(1)}, u32[]{:S(2)}, u32[]{:S(2)}) async-start(f32[32,8,128]{2,1,0:T(8,128)} %broadcast_in_dim_broadcast_in_dim_broadcast_in_dim.6), calls=%async_computation.18 | async-start | bytes 262144 | tf_op jit(solution)/shard_map/all_to_all | solution.py:27
  226.3 6.5 %all-to-all-start.16 = ((bf16[16,96,384]{2,1,0:T(8,128)(2,1)}), bf16[16,96,384]{2,1,0:T(8,128)(2,1)S(1)}, u32[]{:S(2)}, u32[]{:S(2)}) async-start(bf16[16,96,384]{2,1,0:T(8,128)(2,1)} %broadcast_in_dim.139), calls=%async_computation.16 | async-start | bytes 2359296 | tf_op jit(solution)/shard_map/all_to_all | solution.py:27
  258.7 6.5 %all-to-all-start.14 = ((bf16[8,96,768]{2,1,0:T(8,128)(2,1)}), bf16[8,96,768]{2,1,0:T(8,128)(2,1)}, u32[]{:S(2)}, u32[]{:S(2)}) async-start(bf16[8,96,768]{2,1,0:T(8,128)(2,1)} %broadcast_in_dim.136), calls=%async_computation.14 | async-start | bytes 2359296 | tf_op jit(solution)/shard_map/all_to_all | solution.py:27
  273.1 9.2 %all-to-all-done.14 = bf16[8,96,768]{2,1,0:T(8,128)(2,1)} async-done(((bf16[8,96,768]{2,1,0:T(8,128)(2,1)}), bf16[8,96,768]{2,1,0:T(8,128)(2,1)}, u32[]{:S(2)}, u32[]{:S(2)}) %all-to-all-start.14) | async-done | bytes 1179680 | tf_op jit(solution)/shard_map/all_to_all | solution.py:27
  289.4 5.7 %all-to-all-done.19 = f32[8,8,128]{2,1,0:T(8,128)} async-done(((f32[8,8,128]{2,1,0:T(8,128)}), f32[8,8,128]{2,1,0:T(8,128)}, u32[]{:S(2)}, u32[]{:S(2)}) %all-to-all-start.19) | async-done | bytes 32800 | tf_op jit(solution)/shard_map/all_to_all | solution.py:27
  306.5 5.2 %all-to-all-done.17 = bf16[8,96,384]{2,1,0:T(8,128)(2,1)} async-done(((bf16[8,96,384]{2,1,0:T(8,128)(2,1)}), bf16[8,96,384]{2,1,0:T(8,128)(2,1)}, u32[]{:S(2)}, u32[]{:S(2)}) %all-to-all-start.17) | async-done | bytes 589856 | tf_op jit(solution)/shard_map/all_to_all | solution.py:27
  311.7 5.0 %all-to-all-start.6 = ((f32[8,24,384]{2,1,0:T(8,128)}), f32[8,24,384]{2,1,0:T(8,128)S(1)}, u32[]{:S(2)}, u32[]{:S(2)}) async-start(f32[8,24,384]{2,1,0:T(8,128)} %fusion.38), calls=%async_computation.6 | async-start | bytes 589824 | tf_op jit(solution)/shard_map/all_to_all | solution.py:27
  319.9 5.1 %all-to-all-done.6 = f32[8,24,384]{2,1,0:T(8,128)S(1)} async-done(((f32[8,24,384]{2,1,0:T(8,128)}), f32[8,24,384]{2,1,0:T(8,128)S(1)}, u32[]{:S(2)}, u32[]{:S(2)}) %all-to-all-start.6) | async-done | bytes 294944 | tf_op jit(solution)/shard_map/all_to_all | solution.py:27
  329.7 10.2 %all-to-all-done.20 = bf16[8,96,384]{2,1,0:T(8,128)(2,1)S(1)} async-done(((bf16[8,96,384]{2,1,0:T(8,128)(2,1)}), bf16[8,96,384]{2,1,0:T(8,128)(2,1)S(1)}, u32[]{:S(2)}, u32[]{:S(2)}) %all-to-all-start.20) | async-done | bytes 589856 | tf_op jit(solution)/shard_map/all_to_all | solution.py:27
  340.8 13.4 %all-to-all-start.7 = ((bf16[16,2,12,384]{3,1,2,0:T(2,128)(2,1)}), bf16[16,2,12,384]{3,1,2,0:T(2,128)(2,1)S(1)}, u32[]{:S(2)}, u32[]{:S(2)}) async-start(bf16[16,2,12,384]{3,1,2,0:T(2,128)(2,1)} %broadcast_in_dim.127), calls=%async_computation.7 | async-start | bytes 589824 | tf_op jit(solution)/shard_map/all_to_all | solution.py:27
  356.3 5.8 %all-to-all-done.7 = bf16[16,2,12,384]{3,1,2,0:T(2,128)(2,1)S(1)} async-done(((bf16[16,2,12,384]{3,1,2,0:T(2,128)(2,1)}), bf16[16,2,12,384]{3,1,2,0:T(2,128)(2,1)S(1)}, u32[]{:S(2)}, u32[]{:S(2)}) %all-to-all-start.7) | async-done | bytes 294944 | tf_op jit(solution)/shard_map/all_to_all | solution.py:27
  373.0 8.2 %collective-permute-start.8 = (bf16[16,2,12,384]{3,1,2,0:T(2,128)(2,1)S(1)}, bf16[16,2,12,384]{3,1,2,0:T(2,128)(2,1)S(1)}, u32[]{:S(2)}, u32[]{:S(2)}) collective-permute-start(bf16[16,2,12,384]{3,1,2,0:T(2,128)(2,1)S(1)} %copy-done.10), channel_id=1, source_target_pairs={{0,1},{1,0},{2,3},{3,2},{4,5},{5,4},{6,7},{7,6},{8,9},{9,8},{10,11... | collective-permute-start | bytes 884744 | tf_op jit(solution)/shard_map/ppermute | solution.py:35
  381.2 8.3 %collective-permute-start.15 = (bf16[1536,384]{1,0:T(8,128)(2,1)S(1)}, bf16[1536,384]{1,0:T(8,128)(2,1)S(1)}, u32[]{:S(2)}, u32[]{:S(2)}) collective-permute-start(bf16[1536,384]{1,0:T(8,128)(2,1)S(1)} %bitcast.281), channel_id=1, source_target_pairs={{0,1},{1,0},{2,3},{3,2},{4,5},{5,4},{6,7},{7,6},{8,9},{9,8},{10,11... | collective-permute-start | bytes 3538952 | tf_op jit(solution)/shard_map/ppermute | solution.py:35
  400.5 7.8 %fusion.81 = (bf16[768,768]{1,0:T(8,128)(2,1)}, f32[768,768]{1,0:T(8,128)}) fusion(f32[768,768]{1,0:T(8,128)} %get-tuple-element.62, f32[]{:T(128)S(6)} %sqrt.10), kind=kOutput, calls=%fused_computation.186 | convolution fusion | flops 1817837568 | bytes 5898244 | tf_op jit(solution)/shard_map/dot_general | solution.py:68
  409.5 5.9 %all-to-all-done.22 = bf16[8,96,384]{2,1,0:T(8,128)(2,1)S(1)} async-done(((bf16[8,96,384]{2,1,0:T(8,128)(2,1)}), bf16[8,96,384]{2,1,0:T(8,128)(2,1)S(1)}, u32[]{:S(2)}, u32[]{:S(2)}) %all-to-all-start.22) | async-done | bytes 589856 | tf_op jit(solution)/shard_map/all_to_all | solution.py:27
  435.7 5.7 %collective-permute-done.9 = f32[24,384]{1,0:T(8,128)S(1)} collective-permute-done((f32[24,384]{1,0:T(8,128)S(1)}, f32[24,384]{1,0:T(8,128)S(1)}, u32[]{:S(2)}, u32[]{:S(2)}) %collective-permute-start.9) | collective-permute-done | bytes 36896 | tf_op jit(solution)/shard_map/ppermute | solution.py:48
  448.1 7.1 %collective-permute-done.16 = f32[48,384]{1,0:T(8,128)S(1)} collective-permute-done((f32[48,384]{1,0:T(8,128)S(1)}, f32[48,384]{1,0:T(8,128)S(1)}, u32[]{:S(2)}, u32[]{:S(2)}) %collective-permute-start.16) | collective-permute-done | bytes 73760 | tf_op jit(solution)/shard_map/ppermute | solution.py:48
  (235 shorter events, 203.1 us)
Async XLA Ops:
  11.5 15.7 %all-to-all-start.8 = ((bf16[8,12,768]{2,1,0:T(8,128)(2,1)}), bf16[8,12,768]{2,1,0:T(8,128)(2,1)S(1)}, u32[]{:S(2)}, u32[]{:S(2)}) async-start(bf16[8,12,768]{2,1,0:T(8,128)(2,1)} %broadcast_in_dim.128), calls=%async_computation.8 | async-start | bytes 393216 | tf_op jit(solution)/shard_map/all_to_all | solution.py:27
  28.0 11.9 %all-to-all-start.1 = ((bf16[8,12,768]{2,1,0:T(8,128)(2,1)}), bf16[8,12,768]{2,1,0:T(8,128)(2,1)S(1)}, u32[]{:S(2)}, u32[]{:S(2)}) async-start(bf16[8,12,768]{2,1,0:T(8,128)(2,1)} %broadcast_in_dim.56), calls=%async_computation.1 | async-start | bytes 393216 | tf_op jit(solution)/shard_map/all_to_all | solution.py:27
  41.0 22.4 %all-to-all-start.9 = ((bf16[8,96,768]{2,1,0:T(8,128)(2,1)}), bf16[8,96,768]{2,1,0:T(8,128)(2,1)S(1)}, u32[]{:S(2)}, u32[]{:S(2)}) async-start(bf16[8,96,768]{2,1,0:T(8,128)(2,1)} %broadcast_in_dim.130), calls=%async_computation.9 | async-start | bytes 2359296 | tf_op jit(solution)/shard_map/all_to_all | solution.py:27
  64.1 11.8 %all-to-all-start.11 = ((bf16[8,96,48]{1,2,0:T(8,128)(2,1)}), bf16[8,96,48]{1,2,0:T(8,128)(2,1)S(1)}, u32[]{:S(2)}, u32[]{:S(2)}) async-start(bf16[8,96,48]{1,2,0:T(8,128)(2,1)} %bitcast.45), calls=%async_computation.11 | async-start | bytes 196608 | tf_op jit(solution)/shard_map/all_to_all | solution.py:27
  84.0 18.3 %all-to-all-start.3 = ((bf16[8,48,384]{2,1,0:T(8,128)(2,1)}), bf16[8,48,384]{2,1,0:T(8,128)(2,1)S(1)}, u32[]{:S(2)}, u32[]{:S(2)}) async-start(bf16[8,48,384]{2,1,0:T(8,128)(2,1)} %broadcast_in_dim.60), calls=%async_computation.3 | async-start | bytes 589824 | tf_op jit(solution)/shard_map/all_to_all | solution.py:27
  87.4 13.8 %collective-permute-start.2 = (bf16[48,384]{1,0:T(8,128)(2,1)S(1)}, bf16[48,384]{1,0:T(8,128)(2,1)S(1)}, u32[]{:S(2)}, u32[]{:S(2)}) collective-permute-start(bf16[48,384]{1,0:T(8,128)(2,1)S(1)} %get-tuple-element.51), channel_id=1, source_target_pairs={{0,0},{1,16},{8,8},{9,24},{16,1},{17,17},{24,9},{25,25},{2,2},{3,1... | collective-permute-start | bytes 110600 | tf_op jit(solution)/shard_map/ppermute | solution.py:48
  109.9 25.0 %all-to-all-start.4 = ((bf16[16,96,384]{2,1,0:T(8,128)(2,1)}), bf16[16,96,384]{2,1,0:T(8,128)(2,1)S(1)}, u32[]{:S(2)}, u32[]{:S(2)}) async-start(bf16[16,96,384]{2,1,0:T(8,128)(2,1)} %broadcast_in_dim.124), calls=%async_computation.4 | async-start | bytes 2359296 | tf_op jit(solution)/shard_map/all_to_all | solution.py:27
  136.0 20.4 %all-to-all-start.2 = ((bf16[8,96,768]{2,1,0:T(8,128)(2,1)}), bf16[8,96,768]{2,1,0:T(8,128)(2,1)S(1)}, u32[]{:S(2)}, u32[]{:S(2)}) async-start(bf16[8,96,768]{2,1,0:T(8,128)(2,1)} %broadcast_in_dim.58), calls=%async_computation.2 | async-start | bytes 2359296 | tf_op jit(solution)/shard_map/all_to_all | solution.py:27
  139.6 33.8 %collective-permute-start.4 = (bf16[16,96,384]{2,1,0:T(8,128)(2,1)S(1)}, bf16[16,96,384]{2,1,0:T(8,128)(2,1)}, u32[]{:S(2)}, u32[]{:S(2)}) collective-permute-start(bf16[16,96,384]{2,1,0:T(8,128)(2,1)S(1)} %all-to-all-done.4), channel_id=1, source_target_pairs={{0,1},{1,0},{2,3},{3,2},{4,5},{5,4},{6,7},{7,6},{8,9},{9,8},{10,11... | collective-permute-start | bytes 3538952 | tf_op jit(solution)/shard_map/ppermute | solution.py:35
  146.4 14.2 %collective-permute-start.12 = (bf16[48,384]{1,0:T(8,128)(2,1)S(1)}, bf16[48,384]{1,0:T(8,128)(2,1)S(1)}, u32[]{:S(2)}, u32[]{:S(2)}) collective-permute-start(bf16[48,384]{1,0:T(8,128)(2,1)S(1)} %get-tuple-element.43), channel_id=1, source_target_pairs={{0,0},{1,16},{8,8},{9,24},{16,1},{17,17},{24,9},{25,25},{2,2},{3,1... | collective-permute-start | bytes 110600 | tf_op jit(solution)/shard_map/ppermute | solution.py:48
  150.1 10.5 %collective-permute-start.13 = (bf16[48,384]{1,0:T(8,128)(2,1)S(1)}, bf16[48,384]{1,0:T(8,128)(2,1)S(1)}, u32[]{:S(2)}, u32[]{:S(2)}) collective-permute-start(bf16[48,384]{1,0:T(8,128)(2,1)S(1)} %get-tuple-element.44), channel_id=1, source_target_pairs={{0,8},{1,24},{8,0},{9,16},{16,9},{17,25},{24,1},{25,17},{2,10},{3,... | collective-permute-start | bytes 110600 | tf_op jit(solution)/shard_map/ppermute | solution.py:48
  157.2 11.8 %all-to-all-start.13 = ((bf16[8,12,768]{2,1,0:T(8,128)(2,1)}), bf16[8,12,768]{2,1,0:T(8,128)(2,1)S(1)}, u32[]{:S(2)}, u32[]{:S(2)}) async-start(bf16[8,12,768]{2,1,0:T(8,128)(2,1)} %broadcast_in_dim.134), calls=%async_computation.13 | async-start | bytes 393216 | tf_op jit(solution)/shard_map/all_to_all | solution.py:27
  169.9 20.5 %all-to-all-start.15 = ((bf16[8,96,384]{2,1,0:T(8,128)(2,1)}), bf16[8,96,384]{2,1,0:T(8,128)(2,1)S(1)}, u32[]{:S(2)}, u32[]{:S(2)}) async-start(bf16[8,96,384]{2,1,0:T(8,128)(2,1)} %broadcast_in_dim.138), calls=%async_computation.15 | async-start | bytes 1179648 | tf_op jit(solution)/shard_map/all_to_all | solution.py:27
  191.5 15.6 %all-to-all-start.5 = ((bf16[16,2,12,768]{3,1,2,0:T(2,128)(2,1)}), bf16[16,2,12,768]{3,1,2,0:T(2,128)(2,1)}, u32[]{:S(2)}, u32[]{:S(2)}) async-start(bf16[16,2,12,768]{3,1,2,0:T(2,128)(2,1)} %broadcast_in_dim.126), calls=%async_computation.5 | async-start | bytes 1179648 | tf_op jit(solution)/shard_map/all_to_all | solution.py:27
  208.4 16.8 %all-to-all-start.18 = ((f32[32,8,128]{2,1,0:T(8,128)}), f32[32,8,128]{2,1,0:T(8,128)S(1)}, u32[]{:S(2)}, u32[]{:S(2)}) async-start(f32[32,8,128]{2,1,0:T(8,128)} %broadcast_in_dim_broadcast_in_dim_broadcast_in_dim.6), calls=%async_computation.18 | async-start | bytes 262144 | tf_op jit(solution)/shard_map/all_to_all | solution.py:27
  217.1 15.7 %collective-permute-start.6 = (f32[12,384]{1,0:T(8,128)}, f32[12,384]{1,0:T(8,128)}, u32[]{:S(2)}, u32[]{:S(2)}) collective-permute-start(f32[12,384]{1,0:T(8,128)} %get-tuple-element.55), channel_id=1, source_target_pairs={{0,0},{1,16},{8,8},{9,24},{16,1},{17,17},{24,9},{25,25},{2,2},{3,1... | collective-permute-start | bytes 55304 | tf_op jit(solution)/shard_map/ppermute | solution.py:48
  220.6 12.3 %collective-permute-start.7 = (f32[12,384]{1,0:T(8,128)}, f32[12,384]{1,0:T(8,128)}, u32[]{:S(2)}, u32[]{:S(2)}) collective-permute-start(f32[12,384]{1,0:T(8,128)} %get-tuple-element.56), channel_id=1, source_target_pairs={{0,8},{1,24},{8,0},{9,16},{16,9},{17,25},{24,1},{25,17},{2,10},{3,... | collective-permute-start | bytes 55304 | tf_op jit(solution)/shard_map/ppermute | solution.py:48
  224.1 20.1 %collective-permute-start.5 = (bf16[16,2,12,768]{3,1,2,0:T(2,128)(2,1)}, bf16[16,2,12,768]{3,1,2,0:T(2,128)(2,1)}, u32[]{:S(2)}, u32[]{:S(2)}) collective-permute-start(bf16[16,2,12,768]{3,1,2,0:T(2,128)(2,1)} %all-to-all-done.5), channel_id=1, source_target_pairs={{0,1},{1,0},{2,3},{3,2},{4,5},{5,4},{6,7},{7,6},{8,9},{9,8},{10,11... | collective-permute-start | bytes 1769480 | tf_op jit(solution)/shard_map/ppermute | solution.py:35
  226.3 30.4 %all-to-all-start.16 = ((bf16[16,96,384]{2,1,0:T(8,128)(2,1)}), bf16[16,96,384]{2,1,0:T(8,128)(2,1)S(1)}, u32[]{:S(2)}, u32[]{:S(2)}) async-start(bf16[16,96,384]{2,1,0:T(8,128)(2,1)} %broadcast_in_dim.139), calls=%async_computation.16 | async-start | bytes 2359296 | tf_op jit(solution)/shard_map/all_to_all | solution.py:27
  258.7 23.5 %all-to-all-start.14 = ((bf16[8,96,768]{2,1,0:T(8,128)(2,1)}), bf16[8,96,768]{2,1,0:T(8,128)(2,1)}, u32[]{:S(2)}, u32[]{:S(2)}) async-start(bf16[8,96,768]{2,1,0:T(8,128)(2,1)} %broadcast_in_dim.136), calls=%async_computation.14 | async-start | bytes 2359296 | tf_op jit(solution)/shard_map/all_to_all | solution.py:27
  283.5 11.5 %all-to-all-start.19 = ((f32[8,8,128]{2,1,0:T(8,128)}), f32[8,8,128]{2,1,0:T(8,128)}, u32[]{:S(2)}, u32[]{:S(2)}) async-start(f32[8,8,128]{2,1,0:T(8,128)} %broadcast_in_dim_broadcast_in_dim_broadcast_in_dim.7), calls=%async_computation.19 | async-start | bytes 65536 | tf_op jit(solution)/shard_map/all_to_all | solution.py:27
  295.0 16.7 %all-to-all-start.17 = ((bf16[8,96,384]{2,1,0:T(8,128)(2,1)}), bf16[8,96,384]{2,1,0:T(8,128)(2,1)}, u32[]{:S(2)}, u32[]{:S(2)}) async-start(bf16[8,96,384]{2,1,0:T(8,128)(2,1)} %fusion.20), calls=%async_computation.17 | async-start | bytes 1179648 | tf_op jit(solution)/shard_map/all_to_all | solution.py:27
  311.7 13.3 %all-to-all-start.6 = ((f32[8,24,384]{2,1,0:T(8,128)}), f32[8,24,384]{2,1,0:T(8,128)S(1)}, u32[]{:S(2)}, u32[]{:S(2)}) async-start(f32[8,24,384]{2,1,0:T(8,128)} %fusion.38), calls=%async_computation.6 | async-start | bytes 589824 | tf_op jit(solution)/shard_map/all_to_all | solution.py:27
  325.9 14.0 %all-to-all-start.20 = ((bf16[8,96,384]{2,1,0:T(8,128)(2,1)}), bf16[8,96,384]{2,1,0:T(8,128)(2,1)S(1)}, u32[]{:S(2)}, u32[]{:S(2)}) async-start(bf16[8,96,384]{2,1,0:T(8,128)(2,1)} %broadcast_in_dim.140), calls=%async_computation.20 | async-start | bytes 1179648 | tf_op jit(solution)/shard_map/all_to_all | solution.py:27
  340.8 21.3 %all-to-all-start.7 = ((bf16[16,2,12,384]{3,1,2,0:T(2,128)(2,1)}), bf16[16,2,12,384]{3,1,2,0:T(2,128)(2,1)S(1)}, u32[]{:S(2)}, u32[]{:S(2)}) async-start(bf16[16,2,12,384]{3,1,2,0:T(2,128)(2,1)} %broadcast_in_dim.127), calls=%async_computation.7 | async-start | bytes 589824 | tf_op jit(solution)/shard_map/all_to_all | solution.py:27
  363.9 17.3 %all-to-all-start.21 = ((bf16[16,96,384]{2,1,0:T(8,128)(2,1)}), bf16[16,96,384]{2,1,0:T(8,128)(2,1)S(1)}, u32[]{:S(2)}, u32[]{:S(2)}) async-start(bf16[16,96,384]{2,1,0:T(8,128)(2,1)} %broadcast_in_dim.141), calls=%async_computation.21 | async-start | bytes 2359296 | tf_op jit(solution)/shard_map/all_to_all | solution.py:27
  373.0 35.3 %collective-permute-start.8 = (bf16[16,2,12,384]{3,1,2,0:T(2,128)(2,1)S(1)}, bf16[16,2,12,384]{3,1,2,0:T(2,128)(2,1)S(1)}, u32[]{:S(2)}, u32[]{:S(2)}) collective-permute-start(bf16[16,2,12,384]{3,1,2,0:T(2,128)(2,1)S(1)} %copy-done.10), channel_id=1, source_target_pairs={{0,1},{1,0},{2,3},{3,2},{4,5},{5,4},{6,7},{7,6},{8,9},{9,8},{10,11... | collective-permute-start | bytes 884744 | tf_op jit(solution)/shard_map/ppermute | solution.py:35
  381.2 11.9 %collective-permute-start.15 = (bf16[1536,384]{1,0:T(8,128)(2,1)S(1)}, bf16[1536,384]{1,0:T(8,128)(2,1)S(1)}, u32[]{:S(2)}, u32[]{:S(2)}) collective-permute-start(bf16[1536,384]{1,0:T(8,128)(2,1)S(1)} %bitcast.281), channel_id=1, source_target_pairs={{0,1},{1,0},{2,3},{3,2},{4,5},{5,4},{6,7},{7,6},{8,9},{9,8},{10,11... | collective-permute-start | bytes 3538952 | tf_op jit(solution)/shard_map/ppermute | solution.py:35
  396.7 18.7 %all-to-all-start.22 = ((bf16[8,96,384]{2,1,0:T(8,128)(2,1)}), bf16[8,96,384]{2,1,0:T(8,128)(2,1)S(1)}, u32[]{:S(2)}, u32[]{:S(2)}) async-start(bf16[8,96,384]{2,1,0:T(8,128)(2,1)} %fusion.36), calls=%async_computation.22 | async-start | bytes 1179648 | tf_op jit(solution)/shard_map/all_to_all | solution.py:27
  416.4 27.2 %all-to-all-start.23 = ((bf16[8,96,384]{2,1,0:T(8,128)(2,1)}), bf16[8,96,384]{2,1,0:T(8,128)(2,1)}, u32[]{:S(2)}, u32[]{:S(2)}) async-start(bf16[8,96,384]{2,1,0:T(8,128)(2,1)} %broadcast_in_dim.142), calls=%async_computation.23 | async-start | bytes 1179648 | tf_op jit(solution)/shard_map/all_to_all | solution.py:27
  420.9 14.8 %collective-permute-start.10 = (f32[24,384]{1,0:T(8,128)S(1)}, f32[24,384]{1,0:T(8,128)S(1)}, u32[]{:S(2)}, u32[]{:S(2)}) collective-permute-start(f32[24,384]{1,0:T(8,128)S(1)} %get-tuple-element.39), channel_id=1, source_target_pairs={{0,8},{1,24},{8,0},{9,16},{16,9},{17,25},{24,1},{25,17},{2,10},{3,... | collective-permute-start | bytes 110600 | tf_op jit(solution)/shard_map/ppermute | solution.py:48
  425.5 15.9 %collective-permute-start.9 = (f32[24,384]{1,0:T(8,128)S(1)}, f32[24,384]{1,0:T(8,128)S(1)}, u32[]{:S(2)}, u32[]{:S(2)}) collective-permute-start(f32[24,384]{1,0:T(8,128)S(1)} %get-tuple-element.40), channel_id=1, source_target_pairs={{0,0},{1,16},{8,8},{9,24},{16,1},{17,17},{24,9},{25,25},{2,2},{3,1... | collective-permute-start | bytes 110600 | tf_op jit(solution)/shard_map/ppermute | solution.py:48
  (38 other events, 297.0 us)
